TPU v7x, 256 devices: a whole 4x4x8 slice. The times are simulated.
256 devices in a mesh: segment: 2 (over core), et: 128 (over x, y, z).
Axes of the slice: x: 4, y: 4, z: 8, core: 2. Of those that a mesh axis runs over, the one named last changes fastest.
Arguments:
- inputs: bfloat16 [1, 128, 6144], P(None, 'et'), may hold values from -6 to 6
- cotangent: bfloat16 [1, 128, 6144], P(None, 'et'), may hold values from -6 to 6
- gate_weight: bfloat16 [2, 6144, 16384], P('segment', None, 'et'), may hold values from -0.078125 to 0.078125
- up_weight: bfloat16 [2, 6144, 16384], P('segment', None, 'et'), may hold values from -0.078125 to 0.078125
- down_weight: bfloat16 [2, 16384, 6144], P('segment', 'et'), may hold values from -0.0625 to 0.0625
- route_rows: int32 [2, 1, 128], P('segment'), may hold values from 0 to 127, as said below
- route_count: int32 [2, 1], P('segment'), may hold values from 32 to 128, as said below
- route_weight: float32 [2, 1, 128], P('segment'), may hold values from 0.05 to 1
- width_mask: int32 [2, 128], P('segment', 'et'), may hold values from 0 to 1, as said below
Outputs:
- section_output: bfloat16 [2, 1, 128, 6144], P('segment', None, 'et')
- grad_input: bfloat16 [2, 1, 128, 6144], P('segment', None, 'et')
- grad_gate: bfloat16 [2, 6144, 16384], P('segment', None, 'et')
- grad_up: bfloat16 [2, 6144, 16384], P('segment', None, 'et')
- grad_down: bfloat16 [2, 16384, 6144], P('segment', 'et')
Inputs may be any that keep to these rules, and one draw needn't show every extreme that they name: `route_rows`: each list names every one of the 128 tokens once; its first route_count entries are the slots routed to the expert. `route_count`: 128 in at least one entry. `width_mask`: the kept tiles of each section are its first ones, at least 32 of them and never all.
All inputs are finite; a program needn't handle non-finite values.
Results may differ from a plain program's by a relative error of at most 0.015.
Values may be sent and summed in bfloat16 or wider, within the bound.
No kernel may reach another device: no remote copies, remote signals or barrier semaphores. Data moves between devices by JAX's collectives and lax.ppermute only.
A program may use at most 128 MiB of HBM per device.

v0:
```python
import jax
import jax.numpy as jnp
from jax import lax
from jax.sharding import PartitionSpec as P


def shifted(value, axis, by):
    size = lax.axis_size(axis)
    pairs = [(i, i + by) for i in range(size) if 0 <= i + by < size]
    return lax.ppermute(value, axis, pairs)


def expert_hidden(picked, gate_w, up_w, keep):
    gate_value = jnp.dot(picked, gate_w, preferred_element_type=jnp.float32)
    up_value = jnp.dot(picked, up_w, preferred_element_type=jnp.float32)
    hidden = (gate_value * jax.nn.sigmoid(gate_value) * up_value * keep).astype(jnp.bfloat16)
    return (gate_value, up_value, hidden)


def expert_deltas(picked, slot_grad_in, gate_value, up_value, hidden, down_w, keep):
    contract_last = (((1,), (1,)), ((), ()))
    contract_first = (((0,), (0,)), ((), ()))
    hidden_delta = lax.dot_general(
        slot_grad_in, down_w, contract_last, preferred_element_type=jnp.float32
    )
    sig_gate = jax.nn.sigmoid(gate_value)
    gate_delta = (
        hidden_delta * keep * up_value * sig_gate * (1.0 + gate_value * (1.0 - sig_gate))
    ).astype(jnp.bfloat16)
    up_delta = (hidden_delta * keep * gate_value * sig_gate).astype(jnp.bfloat16)
    grad_gate = lax.dot_general(
        picked, gate_delta, contract_first, preferred_element_type=jnp.float32
    )
    grad_up = lax.dot_general(picked, up_delta, contract_first, preferred_element_type=jnp.float32)
    grad_down = lax.dot_general(
        hidden, slot_grad_in, contract_first, preferred_element_type=jnp.float32
    )
    return (gate_delta, up_delta, grad_gate, grad_up, grad_down)


def slot_gradient(gate_delta, up_delta, gate_w, up_w):
    contract_last = (((1,), (1,)), ((), ()))
    slot_grad = lax.dot_general(
        gate_delta, gate_w, contract_last, preferred_element_type=jnp.float32
    )
    return slot_grad + lax.dot_general(
        up_delta, up_w, contract_last, preferred_element_type=jnp.float32
    )


def take_micro(buffer, micro_index):
    return lax.dynamic_index_in_dim(buffer, micro_index, 0, keepdims=False)


def store_micro(buffer, micro_index, value):
    return lax.dynamic_update_index_in_dim(buffer, value, micro_index, 0)


def pick_route(route_rows, route_count, route_weight, micro_index):
    slot_rows = take_micro(route_rows[0], micro_index)
    live_count = take_micro(route_count[0], micro_index)
    slot_weight = take_micro(route_weight[0], micro_index)
    slot_total = slot_rows.shape[0]
    positions = jnp.arange(slot_total, dtype=jnp.int32)
    live = positions < live_count
    inverse = jnp.zeros((slot_total,), jnp.int32).at[slot_rows].set(positions)
    return (slot_rows, jnp.where(live, slot_weight, 0.0), inverse)


def per_device(
    inputs,
    cotangent,
    gate_weight,
    up_weight,
    down_weight,
    route_rows,
    route_count,
    route_weight,
    width_mask,
):
    micro_count = inputs.shape[0]
    token_rows = inputs.shape[1]
    width = inputs.shape[2]
    segment_count = lax.axis_size("segment")
    segment_index = lax.axis_index("segment")
    total_rows = token_rows * lax.axis_size("et")
    slot_count = route_rows.shape[2]
    gate_w = gate_weight[0]
    up_w = up_weight[0]
    down_w = down_weight[0]
    hidden_cols = gate_w.shape[1]
    keep = jnp.repeat(width_mask[0].astype(jnp.float32), hidden_cols // width_mask.shape[1])
    phases = micro_count + segment_count - 1
    saved_input = jnp.zeros((micro_count, token_rows, width), jnp.bfloat16)
    saved_whole = jnp.zeros((micro_count, total_rows, width), jnp.bfloat16)
    saved_gate = jnp.zeros((micro_count, slot_count, hidden_cols), jnp.float32)
    saved_up = jnp.zeros((micro_count, slot_count, hidden_cols), jnp.float32)
    saved_hidden = jnp.zeros((micro_count, slot_count, hidden_cols), jnp.bfloat16)
    outputs = jnp.zeros((micro_count, token_rows, width), jnp.bfloat16)
    incoming = jnp.zeros((token_rows, width), jnp.bfloat16)
    for phase in range(phases):
        micro_raw = phase - segment_index
        valid = (micro_raw >= 0) & (micro_raw < micro_count)
        micro_index = jnp.clip(micro_raw, 0, micro_count - 1)
        current = jnp.where(segment_index == 0, take_micro(inputs, micro_index), incoming)
        gathered = lax.all_gather(current, "et", axis=0, tiled=True)
        slot_rows, slot_scale, inverse = pick_route(
            route_rows, route_count, route_weight, micro_index
        )
        picked = jnp.take(gathered, slot_rows, axis=0)
        gate_value, up_value, hidden = expert_hidden(picked, gate_w, up_w, keep)
        outcome = jnp.dot(hidden, down_w, preferred_element_type=jnp.float32)
        added = jnp.take(slot_scale[:, None] * outcome, inverse, axis=0)
        mine = lax.psum_scatter(added, "et", scatter_dimension=0, tiled=True)
        result = (current.astype(jnp.float32) + mine).astype(jnp.bfloat16)
        late = micro_raw >= 0
        stored = jnp.where(late, micro_index, micro_count - 1)
        saved_input = store_micro(saved_input, stored, current)
        saved_whole = store_micro(saved_whole, stored, gathered)
        saved_gate = store_micro(saved_gate, stored, gate_value)
        saved_up = store_micro(saved_up, stored, up_value)
        saved_hidden = store_micro(saved_hidden, stored, hidden)
        outputs = jnp.where(valid, store_micro(outputs, micro_index, result), outputs)
        if phase + 1 < phases:
            incoming = shifted(result, "segment", 1)
    acc_gate = jnp.zeros((width, hidden_cols), jnp.float32)
    acc_up = jnp.zeros((width, hidden_cols), jnp.float32)
    acc_down = jnp.zeros((hidden_cols, width), jnp.float32)
    grad_inputs = jnp.zeros((micro_count, token_rows, width), jnp.bfloat16)
    incoming = jnp.zeros((token_rows, width), jnp.bfloat16)
    for phase in range(phases):
        micro_raw = phase - (segment_count - 1 - segment_index)
        valid = (micro_raw >= 0) & (micro_raw < micro_count)
        micro_index = jnp.clip(micro_raw, 0, micro_count - 1)
        upstream = jnp.where(
            segment_index == segment_count - 1, take_micro(cotangent, micro_index), incoming
        )
        grad_gathered = lax.all_gather(upstream, "et", axis=0, tiled=True)
        gathered = take_micro(saved_whole, micro_index)
        slot_rows, slot_scale, inverse = pick_route(
            route_rows, route_count, route_weight, micro_index
        )
        slot_scale = jnp.where(valid, slot_scale, 0.0)
        picked = jnp.take(gathered, slot_rows, axis=0)
        grad_picked = jnp.take(grad_gathered, slot_rows, axis=0)
        slot_grad_in = (slot_scale[:, None] * grad_picked.astype(jnp.float32)).astype(jnp.bfloat16)
        gate_delta, up_delta, part_gate, part_up, part_down = expert_deltas(
            picked,
            slot_grad_in,
            take_micro(saved_gate, micro_index),
            take_micro(saved_up, micro_index),
            take_micro(saved_hidden, micro_index),
            down_w,
            keep,
        )
        acc_gate = acc_gate + part_gate
        acc_up = acc_up + part_up
        acc_down = acc_down + part_down
        slot_grad = slot_gradient(gate_delta, up_delta, gate_w, up_w)
        added = jnp.take(slot_grad, inverse, axis=0)
        mine = lax.psum_scatter(added, "et", scatter_dimension=0, tiled=True)
        result = (upstream.astype(jnp.float32) + mine).astype(jnp.bfloat16)
        grad_inputs = jnp.where(valid, store_micro(grad_inputs, micro_index, result), grad_inputs)
        if phase + 1 < phases:
            incoming = shifted(result, "segment", -1)
    return (
        outputs[None],
        grad_inputs[None],
        acc_gate.astype(jnp.bfloat16)[None],
        acc_up.astype(jnp.bfloat16)[None],
        acc_down.astype(jnp.bfloat16)[None],
    )


def solution(mesh):
    return jax.shard_map(
        per_device,
        mesh=mesh,
        in_specs=(
            P(None, "et", None),
            P(None, "et", None),
            P("segment", None, "et"),
            P("segment", None, "et"),
            P("segment", "et", None),
            P("segment", None, None),
            P("segment", None),
            P("segment", None, None),
            P("segment", "et"),
        ),
        out_specs=(
            P("segment", None, "et", None),
            P("segment", None, "et", None),
            P("segment", None, "et"),
            P("segment", None, "et"),
            P("segment", "et", None),
        ),
        check_vma=False,
    )
```

profile of v0, /device:TPU:1, one launch (start us, length us, event | category | flops | bytes accessed | tf_op | source)
XLA Modules:
  0.0 1269.3 jit_solution(9324662932709823214)
XLA Ops:
  7.2 1.5 fusion.56
  10.8 1.0 scatter_custom_fusion
  13.8 113.3 %all-gather.9.cloned.1.call-done = bf16[128,1,6144]{2,1,0:T(2,128)(2,1)} async-done(((bf16[1,1,6144]{2,1,0:T(2,128)(2,1)}), bf16[128,1,6144]{2,1,0:T(2,128)(2,1)}) %all-gather.9.cloned.1.call-update) | async-done | bytes 1572880 | tf_op jit(solution)/shard_map/all_gather | solution.py:106
  127.1 2.8 copy.25
  129.9 2.6 gather_fusion
  132.5 2.6 fusion.24
  135.1 4.2 convolution_multiply_fusion.1
  139.3 6.5 gather_fusion.1
  145.8 4.0 broadcast_select_fusion.3
  151.8 226.8 %all-reduce.9.cloned.1.call-done = f32[128,6144]{1,0:T(8,128)} async-done(((f32[128,6144]{1,0:T(8,128)}), f32[128,6144]{1,0:T(8,128)}) %all-reduce.9.cloned.1.call-update) | async-done | bytes 3145744
  378.6 1.5 fusion.55
  380.1 1.3 collective-permute-start
  381.4 4.8 collective-permute-done
  387.1 108.1 %all-gather.13.cloned.1.call-done = bf16[128,1,6144]{2,1,0:T(2,128)(2,1)} async-done(((bf16[1,1,6144]{2,1,0:T(2,128)(2,1)}), bf16[128,1,6144]{2,1,0:T(2,128)(2,1)}) %all-gather.13.cloned.1.call-update) | async-done | bytes 1572880 | tf_op jit(solution)/shard_map/all_gather | solution.py:138
  495.3 2.8 copy.23
  498.1 2.6 gather_fusion.4
  500.7 111.6 %all-gather.11.cloned.1.call-done = bf16[128,1,6144]{2,1,0:T(2,128)(2,1)} async-done(((bf16[1,1,6144]{2,1,0:T(2,128)(2,1)}), bf16[128,1,6144]{2,1,0:T(2,128)(2,1)}) %all-gather.11.cloned.1.call-update) | async-done | bytes 1572880 | tf_op jit(solution)/shard_map/all_gather | solution.py:106
  612.3 2.8 copy.24
  615.1 2.6 gather_fusion.2
  617.7 2.2 fusion.14
  620.7 0.8 copy-done.4
  623.2 2.3 convolution_add_fusion.4
  625.5 6.5 gather_fusion.5
  632.0 4.0 broadcast_select_fusion.1
  636.0 228.9 %all-reduce.11.cloned.1.call-done = f32[128,6144]{1,0:T(8,128)} async-done(((f32[128,6144]{1,0:T(8,128)}), f32[128,6144]{1,0:T(8,128)}) %all-reduce.11.cloned.1.call-update) | async-done | bytes 3145744
  865.0 1.5 fusion.53
  866.5 6.0 collective-permute-start.1
  872.5 0.8 collective-permute-done.1
  874.3 107.9 %all-gather.15.cloned.1.call-done = bf16[128,1,6144]{2,1,0:T(2,128)(2,1)} async-done(((bf16[1,1,6144]{2,1,0:T(2,128)(2,1)}), bf16[128,1,6144]{2,1,0:T(2,128)(2,1)}) %all-gather.15.cloned.1.call-update) | async-done | bytes 1572880 | tf_op jit(solution)/shard_map/all_gather | solution.py:138
  982.2 2.8 copy.22
  985.0 2.6 gather_fusion.6
  987.6 2.6 multiply_convert_fusion.2
  990.3 2.3 convolution_multiply_fusion
  992.6 6.5 gather_fusion.3
  999.7 2.3 convolution_add_fusion.3
  1002.0 6.4 gather_fusion.7
  1008.4 6.4 broadcast_select_fusion
  1014.8 1.4 copy-done.2
  1016.2 0.7 fusion.68
  1016.9 0.7 fusion.69
  1017.5 0.7 copy-done.9
  1018.3 0.7 fusion.67
  1018.9 0.7 copy-done.10
  1019.7 1.9 fusion.3
  1021.6 1.8 fusion.5
  1023.4 1.8 fusion.4
  1025.3 234.6 %all-reduce.13.cloned.1.call-done = (f32[128,6144]{1,0:T(8,128)}, f32[128,6144]{1,0:T(8,128)}) async-done(((f32[128,6144]{1,0:T(8,128)}, f32[128,6144]{1,0:T(8,128)}), (f32[128,6144]{1,0:T(8,128)}, f32[128,6144]{1,0:T(8,128)})) %all-reduce.13.cloned.1.call-update) | async-done | bytes 6291472
  1259.9 2.6 fusion.50
  (58 shorter events, 9.8 us)
Async XLA Ops:
  7.2 128.0 %copy-start = (bf16[1,6144,128]{2,1,0:T(8,128)(2,1)S(1)}, bf16[1,6144,128]{2,1,0:T(8,128)(2,1)}, u32[]{:S(2)}) copy-start(bf16[1,6144,128]{2,1,0:T(8,128)(2,1)} %param.16) | copy-start | bytes 4718596
  7.2 119.9 %all-gather.9.cloned.1.call-start = ((), (), s32[]{:S(2)}) async-start(), calls=%async_computation | async-start | bytes 3170304 | tf_op jit(solution)/shard_map/all_gather | solution.py:106
  8.7 369.8 %all-reduce.9.cloned.1.call-start = ((), (), s32[]{:S(2)}) async-start(), calls=%async_computation.4 | async-start | bytes 6291456
  132.5 2.6 copy-start.3
  149.8 0.7 copy-start.12
  149.8 1.5 copy-start.13
  149.8 228.8 %copy-start.11 = (bf16[1,1,6144]{2,1,0:T(2,128)(2,1)S(1)}, bf16[1,1,6144]{2,1,0:T(2,128)(2,1)}, u32[]{:S(2)}) copy-start(bf16[1,1,6144]{2,1,0:T(2,128)(2,1)} %param.13) | copy-start | bytes 36868
  149.8 345.5 %all-gather.13.cloned.1.call-start = ((), (), s32[]{:S(2)}) async-start(), calls=%async_computation.2 | async-start | bytes 3170304 | tf_op jit(solution)/shard_map/all_gather | solution.py:138
  151.2 461.2 %all-gather.11.cloned.1.call-start = ((), (), s32[]{:S(2)}) async-start(), calls=%async_computation.1 | async-start | bytes 3170304 | tf_op jit(solution)/shard_map/all_gather | solution.py:106
  380.1 6.1 collective-permute-start
  386.9 478.1 %all-reduce.11.cloned.1.call-start = ((), (), s32[]{:S(2)}) async-start(), calls=%async_computation.5 | async-start | bytes 6291456
  617.7 2.2 copy-start.1
  617.7 2.4 copy-start.6
  620.1 1.4 copy-start.4
  620.1 1.9 copy-start.8
  622.0 0.7 copy-start.14
  636.0 346.2 %all-gather.15.cloned.1.call-start = ((), (), s32[]{:S(2)}) async-start(), calls=%async_computation.3 | async-start | bytes 3170304 | tf_op jit(solution)/shard_map/all_gather | solution.py:138
  866.5 6.9 collective-permute-start.1
  874.0 385.9 %all-reduce.13.cloned.1.call-start = ((), (), s32[]{:S(2)}) async-start(), calls=%async_computation.6 | async-start | bytes 12582912
  987.6 2.7 copy-start.5
  992.6 6.5 copy-start.7
  1014.8 1.4 copy-start.2
  1016.8 1.4 copy-start.9
  1018.3 1.4 copy-start.10
Sparse Core Ops, SparseCore 0:
  12.2 114.7 all-gather.8
  149.9 228.6 all-reduce.8
  383.4 111.7 all-gather.12
  500.0 112.3 all-gather.10
  636.1 228.8 all-reduce.10
  874.2 108.0 all-gather.14
  1014.9 244.9 all-reduce.12
where the time goes:
time: 1270 us
  waiting for transfers between devices  1140 us (90%)
  local copies, waits for them, and re-layouts  54 us (4%)
  matrix products  28.6 us (2%)
  other arithmetic  26 us (2%)
  between operations  15.7 us (1%)
    unnamed x10, waiting for transfers between devices  690 us
    all_gather x2, waiting for transfers between devices, per_device(): gathered = lax.all_gather(current, 'et', axis=0, tiled=True)  225 us
    all_gather x2, waiting for transfers between devices, per_device(): grad_gathered = lax.all_gather(upstream, 'et', axis=0, tiled=True)  216 us
  transfers between devices with their start and end apart: 9, of which 9 were waited for; matrix products, arithmetic and copies ran while one was open for 2% of the time, Pallas kernels for 0%

commit v1 on v0

--- a/solution.py
+++ b/solution.py
@@ -103,7 +103,9 @@
         valid = (micro_raw >= 0) & (micro_raw < micro_count)
         micro_index = jnp.clip(micro_raw, 0, micro_count - 1)
         current = jnp.where(segment_index == 0, take_micro(inputs, micro_index), incoming)
-        gathered = lax.all_gather(current, "et", axis=0, tiled=True)
+        gathered = jnp.concatenate(
+            lax.all_to_all(jnp.stack([current] * lax.axis_size("et")), "et", 0, 0), axis=0
+        )
         slot_rows, slot_scale, inverse = pick_route(
             route_rows, route_count, route_weight, micro_index
         )

time: 1270 us -> 1130 us (0.89)
  waiting for transfers between devices: 1140 us -> 919 us
  starting transfers between devices: 8.01 us -> 35.3 us
  local copies, waits for them, and re-layouts: 54 us -> 79.2 us
  other arithmetic: 26 us -> 44.1 us
    all_gather x2 -> x0, waiting for transfers between devices: 225 us -> none  [per_device(): gathered = lax.all_gather(current, 'et', axis=0, tiled=True)]
    all_to_all x0 -> x2, waiting for transfers between devices: none -> 37.9 us  [per_device(): lax.all_to_all(jnp.stack([current] * lax.axis_size('et')), 'et', 0, 0)]
    all_to_all x0 -> x2, starting transfers between devices: none -> 27.2 us  [per_device(): lax.all_to_all(jnp.stack([current] * lax.axis_size('et')), 'et', 0, 0)]
    all_gather x2, waiting for transfers between devices: 216 us -> 191 us  [per_device(): grad_gathered = lax.all_gather(upstream, 'et', axis=0, tiled=True)]
    another operation x0 -> x2, other arithmetic: none -> 22.5 us  [per_device(): jnp.stack([current] * lax.axis_size('et'))]
    unnamed x35 -> x43, local copies, waits for them, and re-layouts: 16.6 us -> 34.8 us
    unnamed x10 -> x8, waiting for transfers between devices: 690 us -> 685 us
  transfers between devices with their start and end apart: 9 -> 9, of which waited for: 9 -> 8; matrix products, arithmetic and copies ran while one was open for 2% -> 3% of each run, Pallas kernels for 0% -> 0%
where the time goes in v1:
time: 1130 us; the launch traced here: 1120 us
  waiting for transfers between devices  919 us (81%)
  local copies, waits for them, and re-layouts  79.2 us (7%)
  other arithmetic  44.1 us (4%)
  starting transfers between devices  35.3 us (3%)
  matrix products  28.6 us (3%)
  between operations  15.8 us (1%)
    unnamed x8, waiting for transfers between devices  685 us
    all_gather x2, waiting for transfers between devices, per_device(): grad_gathered = lax.all_gather(upstream, 'et', axis=0, tiled=True)  191 us
    all_to_all x2, waiting for transfers between devices, per_device(): lax.all_to_all(jnp.stack([current] * lax.axis_size('et')), 'et', 0, 0)  37.9 us
    unnamed x43, local copies, waits for them, and re-layouts  34.8 us
    all_to_all x2, starting transfers between devices, per_device(): lax.all_to_all(jnp.stack([current] * lax.axis_size('et')), 'et', 0, 0)  27.2 us
  transfers between devices with their start and end apart: 9, of which 8 were waited for; matrix products, arithmetic and copies ran while one was open for 3% of the time, Pallas kernels for 0%

profile of v1, /device:TPU:1, one launch (start us, length us, event | category | flops | bytes accessed | tf_op | source)
XLA Modules:
  0.0 1121.7 jit_solution(10390578793487919213)
XLA Ops:
  7.3 3.3 stack.7
  11.1 11.2 %reduce.4 = bf16[128,6144]{1,0:T(8,128)(2,1)S(1)} reduce(bf16[128,1,6144]{2,1,0:T(2,128)(2,1)} %stack.7, bf16[]{:T(256)} %broadcast.266), dimensions={1}, to_apply=%stack.7.reduce_sub_computation | reduce | bytes 3145730 | tf_op jit(solution)/shard_map/stack | solution.py:107
  22.3 2.1 reshape.326
  24.4 16.7 %all-to-all-start = ((bf16[128,2,3072]{2,1,0:T(2,128)(2,1)}), bf16[128,2,3072]{2,1,0:T(2,128)(2,1)S(1)}, u32[]{:S(2)}, u32[]{:S(2)}) async-start(bf16[128,2,3072]{2,1,0:T(2,128)(2,1)} %reshape.326), calls=%async_computation | async-start | bytes 3145728 | tf_op jit(solution)/shard_map/all_to_all | solution.py:107
  43.5 37.9 %all-to-all-done = bf16[128,2,3072]{2,1,0:T(2,128)(2,1)S(1)} async-done(((bf16[128,2,3072]{2,1,0:T(2,128)(2,1)}), bf16[128,2,3072]{2,1,0:T(2,128)(2,1)S(1)}, u32[]{:S(2)}, u32[]{:S(2)}) %all-to-all-start) | async-done | bytes 1572896 | tf_op jit(solution)/shard_map/all_to_all | solution.py:107
  81.4 3.8 reshape.327
  85.2 2.8 copy.25
  88.0 2.6 gather_fusion
  90.6 2.6 fusion.24
  93.2 4.2 convolution_multiply_fusion.1
  97.4 6.4 gather_fusion.1
  103.9 3.9 broadcast_select_fusion.3
  109.1 221.8 %all-reduce.9.cloned.1.call-done = f32[128,6144]{1,0:T(8,128)} async-done(((f32[128,6144]{1,0:T(8,128)}), f32[128,6144]{1,0:T(8,128)}) %all-reduce.9.cloned.1.call-update) | async-done | bytes 3145744
  330.9 1.6 fusion.53
  332.5 1.7 collective-permute-start
  334.9 3.7 collective-permute-done
  338.7 3.3 stack.8
  342.0 11.2 %reduce.5 = bf16[128,6144]{1,0:T(8,128)(2,1)S(1)} reduce(bf16[128,1,6144]{2,1,0:T(2,128)(2,1)} %stack.8, bf16[]{:T(256)} %broadcast.266), dimensions={1}, to_apply=%stack.8.reduce_sub_computation | reduce | bytes 3145730 | tf_op jit(solution)/shard_map/stack | solution.py:107
  353.2 2.1 reshape.328
  355.3 10.5 all-to-all-start.1
  365.9 83.3 %all-gather.5.cloned.1.call-done = bf16[128,1,6144]{2,1,0:T(2,128)(2,1)} async-done(((bf16[1,1,6144]{2,1,0:T(2,128)(2,1)}), bf16[128,1,6144]{2,1,0:T(2,128)(2,1)}) %all-gather.5.cloned.1.call-update) | async-done | bytes 1572880 | tf_op jit(solution)/shard_map/all_gather | solution.py:140
  449.1 2.8 copy.23
  451.9 2.6 gather_fusion.4
  454.6 10.4 reshape.329
  464.9 2.8 copy.24
  467.7 2.6 gather_fusion.2
  470.3 2.2 fusion.14
  475.8 2.3 convolution_add_fusion.4
  478.1 6.5 gather_fusion.5
  484.5 4.0 broadcast_select_fusion.1
  488.6 228.8 %all-reduce.11.cloned.1.call-done = f32[128,6144]{1,0:T(8,128)} async-done(((f32[128,6144]{1,0:T(8,128)}), f32[128,6144]{1,0:T(8,128)}) %all-reduce.11.cloned.1.call-update) | async-done | bytes 3145744
  717.4 1.6 fusion.57
  719.0 6.0 collective-permute-start.1
  726.8 107.9 %all-gather.7.cloned.1.call-done = bf16[128,1,6144]{2,1,0:T(2,128)(2,1)} async-done(((bf16[1,1,6144]{2,1,0:T(2,128)(2,1)}), bf16[128,1,6144]{2,1,0:T(2,128)(2,1)}) %all-gather.7.cloned.1.call-update) | async-done | bytes 1572880 | tf_op jit(solution)/shard_map/all_gather | solution.py:140
  834.8 2.8 copy.22
  837.5 2.6 gather_fusion.6
  840.2 2.6 multiply_convert_fusion.2
  842.8 2.3 convolution_multiply_fusion
  845.1 6.5 gather_fusion.3
  852.2 2.3 convolution_add_fusion.3
  854.5 6.4 gather_fusion.7
  860.9 6.4 broadcast_select_fusion
  867.3 1.4 copy-done.2
  872.2 1.9 fusion.3
  874.1 1.8 fusion.5
  876.0 1.8 fusion.4
  877.8 234.3 %all-reduce.13.cloned.1.call-done = (f32[128,6144]{1,0:T(8,128)}, f32[128,6144]{1,0:T(8,128)}) async-done(((f32[128,6144]{1,0:T(8,128)}, f32[128,6144]{1,0:T(8,128)}), (f32[128,6144]{1,0:T(8,128)}, f32[128,6144]{1,0:T(8,128)})) %all-reduce.13.cloned.1.call-update) | async-done | bytes 6291472
  1112.1 2.6 fusion.50
  (69 shorter events, 12.9 us)
Async XLA Ops:
  7.2 86.1 %copy-start = (bf16[1,6144,128]{2,1,0:T(8,128)(2,1)S(1)}, bf16[1,6144,128]{2,1,0:T(8,128)(2,1)}, u32[]{:S(2)}) copy-start(bf16[1,6144,128]{2,1,0:T(8,128)(2,1)} %param.16) | copy-start | bytes 4718596
  24.4 18.0 %copy-start.14 = (s32[1,1,128]{2,1,0:T(1,128)S(1)}, s32[1,1,128]{2,1,0:T(1,128)}, u32[]{:S(2)}) copy-start(s32[1,1,128]{2,1,0:T(1,128)} %param.18) | copy-start | bytes 1540
  24.4 19.1 %copy-start.13 = (f32[1,1,128]{2,1,0:T(1,128)S(1)}, f32[1,1,128]{2,1,0:T(1,128)}, u32[]{:S(2)}) copy-start(f32[1,1,128]{2,1,0:T(1,128)} %param.20) | copy-start | bytes 1540
  24.4 57.1 %all-to-all-start = ((bf16[128,2,3072]{2,1,0:T(2,128)(2,1)}), bf16[128,2,3072]{2,1,0:T(2,128)(2,1)S(1)}, u32[]{:S(2)}, u32[]{:S(2)}) async-start(bf16[128,2,3072]{2,1,0:T(2,128)(2,1)} %reshape.326), calls=%async_computation | async-start | bytes 3145728 | tf_op jit(solution)/shard_map/all_to_all | solution.py:107
  41.0 289.8 %all-reduce.9.cloned.1.call-start = ((), (), s32[]{:S(2)}) async-start(), calls=%async_computation.4 | async-start | bytes 6291456
  90.6 2.6 copy-start.3
  107.8 0.7 copy-start.15
  107.8 223.1 %copy-start.11 = (bf16[1,1,6144]{2,1,0:T(2,128)(2,1)S(1)}, bf16[1,1,6144]{2,1,0:T(2,128)(2,1)}, u32[]{:S(2)}) copy-start(bf16[1,1,6144]{2,1,0:T(2,128)(2,1)} %param.13) | copy-start | bytes 36868
  107.8 226.4 %copy-start.12 = (bf16[1,1,6144]{2,1,0:T(2,128)(2,1)S(1)}, bf16[1,1,6144]{2,1,0:T(2,128)(2,1)}, u32[]{:S(2)}) copy-start(bf16[1,1,6144]{2,1,0:T(2,128)(2,1)} %param.14) | copy-start | bytes 36868
  107.8 341.3 %all-gather.5.cloned.1.call-start = ((), (), s32[]{:S(2)}) async-start(), calls=%async_computation.2 | async-start | bytes 3170304 | tf_op jit(solution)/shard_map/all_gather | solution.py:140
  332.5 6.1 collective-permute-start
  355.3 99.3 %all-to-all-start.1 = ((bf16[128,2,3072]{2,1,0:T(2,128)(2,1)}), bf16[128,2,3072]{2,1,0:T(2,128)(2,1)}, u32[]{:S(2)}, u32[]{:S(2)}) async-start(bf16[128,2,3072]{2,1,0:T(2,128)(2,1)} %reshape.328), calls=%async_computation.1 | async-start | bytes 3145728 | tf_op jit(solution)/shard_map/all_to_all | solution.py:107
  365.8 351.6 %all-reduce.11.cloned.1.call-start = ((), (), s32[]{:S(2)}) async-start(), calls=%async_computation.5 | async-start | bytes 6291456
  470.3 2.2 copy-start.1
  470.3 2.4 copy-start.6
  472.7 1.4 copy-start.4
  472.7 1.9 copy-start.8
  474.6 0.7 copy-start.16
  488.5 346.2 %all-gather.7.cloned.1.call-start = ((), (), s32[]{:S(2)}) async-start(), calls=%async_computation.3 | async-start | bytes 3170304 | tf_op jit(solution)/shard_map/all_gather | solution.py:140
  719.0 6.9 collective-permute-start.1
  726.6 385.6 %all-reduce.13.cloned.1.call-start = ((), (), s32[]{:S(2)}) async-start(), calls=%async_computation.6 | async-start | bytes 12582912
  840.2 2.7 copy-start.5
  845.1 6.5 copy-start.7
  867.3 1.4 copy-start.2
  869.4 1.4 copy-start.9
  870.8 1.4 copy-start.10
Sparse Core Ops, SparseCore 0:
  107.9 222.8 all-reduce.8
  335.7 113.3 all-gather.4
  488.7 228.7 all-reduce.10
  726.7 108.0 all-gather.6
  867.4 244.6 all-reduce.12
